TPU v7x, 256 devices: a whole 4x4x8 slice. The times are simulated.
256 devices in a mesh: az: 8 (over z), rng: 8 (over y_lo, x), dp: 4 (over y_hi, core).
Axes of the slice: x: 4, y: 4 (y_hi: 2, y_lo: 2; y = y_hi * 2 + y_lo), z: 8, core: 2. Of those that a mesh axis runs over, the one named last changes fastest.
Arguments:
- tokens: bfloat16 [4, 128, 128, 512], P('dp', 'az', 'rng'), may hold values from -6 to 6
- qkv_weight: bfloat16 [512, 1536], replicated, may hold values from -0.25 to 0.25
- out_weight: bfloat16 [512, 512], replicated, may hold values from -0.25 to 0.25
- relative_bias: float32 [8, 17, 17], replicated, may hold values from -4 to 260
- cotangent: bfloat16 [4, 128, 128, 512], P('dp', 'az', 'rng'), may hold values from -6 to 6
Outputs:
- grad_tokens: bfloat16 [4, 128, 128, 512], P('dp', 'az', 'rng')
- grad_qkv_weight: float32 [512, 1536], P(('az', 'rng'))
- grad_out_weight: float32 [512, 512], P(('az', 'rng'))
- grad_bias: float32 [8, 17, 17], replicated
All inputs are finite; a program needn't handle non-finite values.
Results may differ from a plain program's by a relative error of at most 0.012.
Values may be sent and summed in bfloat16 or wider, within the bound.
No kernel may reach another device: no remote copies, remote signals or barrier semaphores. Data moves between devices by JAX's collectives and lax.ppermute only.
A program may use at most 128 MiB of HBM per device.

v0:
```python
import math
import jax
import jax.numpy as jnp
from jax import lax
from jax.sharding import PartitionSpec as P


def extended(cells, sides, width, closed):
    for axis, dim in sides:
        count = lax.axis_size(axis)
        ends = count if closed else count - 1
        head = lax.slice_in_dim(cells, 0, width, axis=dim)
        tail = lax.slice_in_dim(cells, cells.shape[dim] - width, cells.shape[dim], axis=dim)
        cells = jnp.concatenate(
            [
                lax.ppermute(tail, axis, [(i, (i + 1) % count) for i in range(ends)]),
                cells,
                lax.ppermute(head, axis, [((i + 1) % count, i) for i in range(ends)]),
            ],
            axis=dim,
        )
    return cells


def starts(*values):
    return tuple((jnp.asarray(value).astype(jnp.int32) for value in values))


def selector(length, radius, present):
    span = 2 * radius + 1
    inner = jnp.arange(length)[:, None, None]
    outer = jnp.arange(length + 2 * radius)[None, :, None]
    offset = jnp.arange(span)[None, None, :]
    return ((outer - inner == offset) & present[None, :, None]).astype(jnp.float32)


def window(table, along, across):
    heads = table.shape[0]
    part_bias = jnp.einsum("hxy,jly->hxjl", table, across, precision=lax.Precision.HIGHEST)
    full_bias = jnp.einsum("ikx,hxjl->hijkl", along, part_bias, precision=lax.Precision.HIGHEST)
    row_total = along.shape[0] * across.shape[0]
    col_total = along.shape[1] * across.shape[1]
    inside = (
        jnp.sum(along, axis=2)[:, None, :, None] * jnp.sum(across, axis=2)[None, :, None, :] > 0.5
    )
    return (full_bias.reshape(heads, row_total, col_total), inside.reshape(row_total, col_total))


def bias_grad(d_score, along, across):
    heads = d_score.shape[0]
    shaped = d_score.reshape(
        heads, along.shape[0], across.shape[0], along.shape[1], across.shape[1]
    )
    folded = jnp.einsum("hijkl,ikx->hxjl", shaped, along, precision=lax.Precision.HIGHEST)
    return jnp.einsum("hxjl,jly->hxy", folded, across, precision=lax.Precision.HIGHEST)


def query_side(queries, d_attended, key_rows, value_rows, bias, inside, scale):
    score = (
        jnp.einsum("qhc,khc->hqk", queries, key_rows, preferred_element_type=jnp.float32) * scale
        + bias
    )
    score = jnp.where(inside[None], score, -jnp.inf)
    top = jnp.max(score, axis=2, keepdims=True)
    log_total = top + jnp.log(jnp.sum(jnp.exp(score - top), axis=2, keepdims=True))
    soft_prob = jnp.exp(score - log_total)
    prob_low = soft_prob.astype(jnp.bfloat16)
    attended = jnp.einsum(
        "hqk,khc->qhc", prob_low, value_rows, preferred_element_type=jnp.float32
    ).astype(jnp.bfloat16)
    delta = jnp.einsum("qhc,qhc->hq", d_attended, attended, preferred_element_type=jnp.float32)
    d_prob = jnp.einsum("qhc,khc->hqk", d_attended, value_rows, preferred_element_type=jnp.float32)
    d_score = soft_prob * (d_prob - delta[:, :, None])
    score_low = d_score.astype(jnp.bfloat16)
    d_query = (
        jnp.einsum("hqk,khc->qhc", score_low, key_rows, preferred_element_type=jnp.float32) * scale
    ).astype(jnp.bfloat16)
    return (attended, log_total[:, :, 0], delta, d_query, d_score, score_low, prob_low)


def shards(tokens, qkv_weight, out_weight, relative_bias, cotangent):
    sweeps, azimuth, radial, width = tokens.shape
    heads = relative_bias.shape[0]
    radius = relative_bias.shape[1] // 2
    head_dim = width // heads
    scale = 1.0 / math.sqrt(head_dim)
    local_count = sweeps * azimuth * radial
    flat_tokens = tokens.reshape(local_count, width)
    flat_cot = cotangent.reshape(local_count, width)
    projected = jnp.dot(flat_tokens, qkv_weight, preferred_element_type=jnp.float32).astype(
        jnp.bfloat16
    )
    projected = projected.reshape(sweeps, azimuth, radial, 3 * width)
    queries = projected[..., :width]
    key_value = projected[..., width:]
    d_attended = lax.dot_general(
        flat_cot, out_weight, (((1,), (1,)), ((), ())), preferred_element_type=jnp.float32
    )
    d_attended = d_attended.astype(jnp.bfloat16).reshape(sweeps, azimuth, radial, width)
    key_ext = extended(key_value, (("az", 1), ("rng", 2)), radius, True)
    tile_side = 8
    tiles_az = azimuth // tile_side
    tiles_rg = radial // tile_side
    tile_count = sweeps * tiles_az * tiles_rg
    group = math.gcd(tile_count, 8)
    turns = tile_count // group
    ext_side = tile_side + 2 * radius
    tile_cells = tile_side * tile_side
    ext_cells = ext_side * ext_side
    first_col = lax.axis_index("rng") * radial
    total_cols = lax.axis_size("rng") * radial
    every_col = jnp.ones((ext_side,), dtype=bool)
    along = selector(tile_side, radius, every_col)
    bias_fixed, inside_fixed = window(relative_bias, along, along)

    def locate(counter):
        sweep_at = counter // (tiles_az * tiles_rg)
        leftover = counter % (tiles_az * tiles_rg)
        return (sweep_at, leftover // tiles_rg * tile_side, leftover % tiles_rg * tile_side)

    def inside_of(col_at):
        column = first_col + col_at - radius + jnp.arange(ext_side)
        present = (column >= 0) & (column < total_cols)
        present_cells = jnp.broadcast_to(present[None, :], (ext_side, ext_side)).reshape(ext_cells)
        return inside_fixed & present_cells[None, :]

    def untile(leaf):
        last = leaf.shape[-1]
        shaped = leaf.reshape(sweeps, tiles_az, tiles_rg, tile_side, tile_side, last)
        return shaped.transpose(0, 1, 3, 2, 4, 5).reshape(sweeps, azimuth, radial, last)

    def query_tile(counter):
        sweep_at, row_at, col_at = locate(counter)
        place = starts(sweep_at, row_at, col_at, 0)
        query_block = lax.dynamic_slice(queries, place, (1, tile_side, tile_side, width)).reshape(
            tile_cells, heads, head_dim
        )
        cot_block = lax.dynamic_slice(d_attended, place, (1, tile_side, tile_side, width)).reshape(
            tile_cells, heads, head_dim
        )
        pair_block = lax.dynamic_slice(key_ext, place, (1, ext_side, ext_side, 2 * width)).reshape(
            ext_cells, 2, heads, head_dim
        )
        inside = inside_of(col_at)
        attended, log_total, delta, d_query, d_score, score_low, prob_low = query_side(
            query_block, cot_block, pair_block[:, 0], pair_block[:, 1], bias_fixed, inside, scale
        )
        d_key = (
            jnp.einsum("hqk,qhc->khc", score_low, query_block, preferred_element_type=jnp.float32)
            * scale
        )
        d_value = jnp.einsum(
            "hqk,qhc->khc", prob_low, cot_block, preferred_element_type=jnp.float32
        )
        term = jnp.stack([d_key, d_value], axis=1).reshape(1, ext_side, ext_side, 2 * width)
        return (
            attended.reshape(tile_cells, width),
            log_total.T,
            delta.T,
            d_query.reshape(tile_cells, width),
            d_score,
            term,
        )

    sums_init = jnp.zeros(
        (sweeps, azimuth + 2 * radius, radial + 2 * radius, 2 * width), jnp.float32
    )

    def query_turn(carry, counter):
        part_sums, score_sum = carry
        lanes = counter * group + jnp.arange(group, dtype=jnp.int32)
        attended, log_total, delta, d_query, d_scores, terms = jax.vmap(query_tile)(lanes)
        score_sum = score_sum + jnp.sum(d_scores, axis=0)
        for member in range(group):
            sweep_at, row_at, col_at = locate(lanes[member])
            place = starts(sweep_at, row_at, col_at, 0)
            current = lax.dynamic_slice(part_sums, place, terms[member].shape)
            part_sums = lax.dynamic_update_slice(part_sums, current + terms[member], place)
        return ((part_sums, score_sum), (attended, log_total, delta, d_query))

    init = (sums_init, jnp.zeros((heads, tile_cells, ext_cells), jnp.float32))
    (part_sums, score_total), outputs = lax.scan(
        query_turn, init, jnp.arange(turns, dtype=jnp.int32)
    )
    bias_local = bias_grad(score_total, along, along)
    attended_all, log_all, delta_all, dquery_all = [
        untile(leaf.reshape((tile_count,) + leaf.shape[2:])) for leaf in outputs
    ]
    edge_terms = jnp.concatenate(
        [part_sums[:, :, :radius], part_sums[:, :, radial + radius :]], axis=2
    )
    arrived = extended(edge_terms.astype(jnp.bfloat16), (("rng", 2),), radius, False).astype(
        edge_terms.dtype
    )
    inner = part_sums[:, :, radius : radius + radial]
    inner = inner.at[:, :, :radius].add(arrived[:, :, :radius])
    inner = inner.at[:, :, radial - radius :].add(arrived[:, :, 3 * radius :])
    cycle_terms = jnp.concatenate([inner[:, :radius], inner[:, azimuth + radius :]], axis=1)
    arrived_cycle = extended(cycle_terms.astype(jnp.bfloat16), (("az", 1),), radius, True).astype(
        cycle_terms.dtype
    )
    owned = inner[:, radius : radius + azimuth]
    owned = owned.at[:, :radius].add(arrived_cycle[:, :radius])
    owned = owned.at[:, azimuth - radius :].add(arrived_cycle[:, 3 * radius :])
    grad_pair = owned.astype(jnp.bfloat16)
    grad_qkv = jnp.concatenate([dquery_all, grad_pair], axis=3)
    grad_flat = grad_qkv.reshape(local_count, 3 * width)
    grad_tokens = lax.dot_general(
        grad_flat, qkv_weight, (((1,), (1,)), ((), ())), preferred_element_type=jnp.float32
    )
    grad_tokens = grad_tokens.astype(jnp.bfloat16).reshape(sweeps, azimuth, radial, width)
    local_qkv = lax.dot_general(
        flat_tokens, grad_flat, (((0,), (0,)), ((), ())), preferred_element_type=jnp.float32
    )
    local_out = lax.dot_general(
        attended_all.reshape(local_count, width),
        flat_cot,
        (((0,), (0,)), ((), ())),
        preferred_element_type=jnp.float32,
    )
    share = width // (lax.axis_size("az") * lax.axis_size("rng"))
    total_qkv, total_out, total_bias = lax.psum(
        (local_qkv, local_out, bias_local), ("az", "rng", "dp")
    )
    first_row = lax.axis_index(("az", "rng")) * share
    rows_qkv = lax.dynamic_slice_in_dim(total_qkv, first_row, share, 0)
    rows_out = lax.dynamic_slice_in_dim(total_out, first_row, share, 0)
    return (grad_tokens, rows_qkv, rows_out, total_bias)


def solution(mesh):
    placed = (P("dp", "az", "rng", None), P(), P(), P(), P("dp", "az", "rng", None))
    return jax.shard_map(
        shards,
        mesh=mesh,
        in_specs=placed,
        out_specs=(P("dp", "az", "rng", None), P(("az", "rng"), None), P(("az", "rng"), None), P()),
        check_vma=False,
    )
```

profile of v0, /device:TPU:97, one launch (start us, length us, event | category | flops | bytes accessed | tf_op | source)
XLA Modules:
  0.0 517.0 jit_solution(8498767762918409143)
XLA Ops:
  8.6 1.5 convolution_convert_fusion
  11.0 2.8 collective-permute-start
  24.8 8.0 %while.16 = (s32[]{:T(128)}, bf16[1,16,16,512]{3,2,1,0:T(8,128)(2,1)S(1)}, s32[4,4]{1,0:T(4,128)S(1)}, bf16[4,1,8,8,512]{4,3,2,1,0:T(8,128)(2,1)S(1)}, s32[]{:T(128)}) while((s32[]{:T(128)}, bf16[1,16,16,512]{3,2,1,0:T(8,128)(2,1)S(1)}, s32[4,4]{1,0:T(4,128)S(1)}, bf16[4,1,8,8,512]{4,3,2,1,0:T(8,128)(2,1)S(1)}, s32[]{:T(128)}) %tuple.101), condition=%wide.while_cond.6, body=%wide.while_body.6.sunk | while | flops 2 | bytes 131205 | solution.py:138
  34.2 8.3 %while.15 = (s32[]{:T(128)}, bf16[1,16,16,512]{3,2,1,0:T(8,128)(2,1)S(1)}, s32[4,4]{1,0:T(4,128)S(1)}, bf16[4,1,8,8,512]{4,3,2,1,0:T(8,128)(2,1)S(1)}, s32[]{:T(128)}) while((s32[]{:T(128)}, bf16[1,16,16,512]{3,2,1,0:T(8,128)(2,1)S(1)}, s32[4,4]{1,0:T(4,128)S(1)}, bf16[4,1,8,8,512]{4,3,2,1,0:T(8,128)(2,1)S(1)}, s32[]{:T(128)}) %tuple.102), condition=%wide.while_cond.5, body=%wide.while_body.5.sunk | while | flops 2 | bytes 131205 | solution.py:135
  43.6 2.6 copy.46
  50.8 2.8 collective-permute-start.3
  53.6 4.6 convolution_bitcast_fusion.1
  58.3 6.6 %copy.22 = f32[8,8,8,24,24]{4,3,2,1,0:T(8,128)} copy(f32[8,8,8,24,24]{3,4,1,2,0:T(8,128)} %convolution_bitcast_fusion.1) | data formatting | bytes 2359296 | tf_op jit(solution)/shard_map/ikx,hxjl->hijkl/transpose | solution.py:40
  64.8 4.3 add.387
  70.0 2.8 pad_maximum_fusion.1
  72.8 19.3 %while.14 = (s32[]{:T(128)}, bf16[1,32,32,1024]{3,2,1,0:T(8,128)(2,1)}, s32[4,4]{1,0:T(4,128)S(1)}, bf16[4,1,24,24,1024]{4,3,2,1,0:T(8,128)(2,1)}, s32[]{:T(128)}) while((s32[]{:T(128)}, bf16[1,32,32,1024]{3,2,1,0:T(8,128)(2,1)}, s32[4,4]{1,0:T(4,128)S(1)}, bf16[4,1,24,24,1024]{4,3,2,1,0:T(8,128)(2,1)}, s32[]{:T(128)}) %tuple.95), condition=%wide.while_cond.4, body=%wide.while_body.4.sunk | while | flops 2 | bytes 2360445 | solution.py:141
  73.4 4.3 bitcast_dynamic-update-slice_fusion.6
  78.2 4.2 bitcast_dynamic-update-slice_fusion.6
  83.0 4.3 bitcast_dynamic-update-slice_fusion.6
  87.9 4.2 bitcast_dynamic-update-slice_fusion.6
  92.1 13.1 %reshape.627 = bf16[4,576,2,8,64]{4,3,2,1,0:T(8,128)(2,1)} reshape(bf16[4,1,24,24,1024]{4,3,2,1,0:T(8,128)(2,1)} %get-tuple-element.92) | data formatting | bytes 9437184 | tf_op jit(solution)/shard_map/while/body/eval_jaxpr/vmap()/reshape | solution.py:141
  105.2 8.1 %fusion.80 = (bf16[4,576,1,8,64]{4,3,2,1,0:T(8,128)(2,1)}, bf16[4,576,1,8,64]{4,3,2,1,0:T(8,128)(2,1)}) fusion(bf16[4,576,2,8,64]{4,3,2,1,0:T(8,128)(2,1)} %reshape.627), kind=kLoop, calls=%fused_computation.139 | loop fusion | bytes 9437184 | tf_op jit(solution)/shard_map/while/body/eval_jaxpr/vmap()/slice | solution.py:146
  113.3 6.2 %copy.51 = bf16[4,576,1,8,64]{1,4,3,0,2:T(8,128)(2,1)} copy(bf16[4,576,1,8,64]{4,3,2,1,0:T(8,128)(2,1)} %get-tuple-element.153) | data formatting | bytes 4718592
  119.5 6.2 %copy.50 = bf16[4,576,1,8,64]{1,4,3,0,2:T(8,128)(2,1)} copy(bf16[4,576,1,8,64]{4,3,2,1,0:T(8,128)(2,1)} %get-tuple-element.154) | data formatting | bytes 4718592
  125.8 3.1 fusion.86
  128.9 1.5 exponential_reduce_fusion
  132.4 2.1 multiply_reduce_fusion
  134.5 2.1 fusion.87
  138.2 4.6 pad_maximum_fusion
  142.8 5.8 %copy.32 = f32[1,576,2,8,64]{4,3,2,1,0:T(8,128)} copy(f32[1,576,2,8,64]{1,4,3,0,2:T(8,128)} %get-tuple-element.149) | data formatting | bytes 4718592 | tf_op jit(solution)/shard_map/while/body/eval_jaxpr/slice | solution.py:178
  148.6 5.0 squeeze.52
  153.6 5.8 %copy.29 = f32[1,576,2,8,64]{4,3,2,1,0:T(8,128)} copy(f32[1,576,2,8,64]{1,4,3,0,2:T(8,128)} %get-tuple-element.150) | data formatting | bytes 4718592 | tf_op jit(solution)/shard_map/while/body/eval_jaxpr/slice | solution.py:178
  159.4 5.0 squeeze.45
  164.4 5.8 %copy.30 = f32[1,576,2,8,64]{4,3,2,1,0:T(8,128)} copy(f32[1,576,2,8,64]{1,4,3,0,2:T(8,128)} %get-tuple-element.151) | data formatting | bytes 4718592 | tf_op jit(solution)/shard_map/while/body/eval_jaxpr/slice | solution.py:178
  170.2 5.0 squeeze.48
  175.2 5.8 %copy.31 = f32[1,576,2,8,64]{4,3,2,1,0:T(8,128)} copy(f32[1,576,2,8,64]{1,4,3,0,2:T(8,128)} %get-tuple-element.152) | data formatting | bytes 4718592 | tf_op jit(solution)/shard_map/while/body/eval_jaxpr/slice | solution.py:178
  180.9 5.0 squeeze.50
  187.9 1.4 copy-done.7
  194.4 2.1 collective-permute-start.4
  197.8 1.4 slice.323
  202.4 4.3 fusion.29
  211.5 2.5 fusion.35
  214.0 2.6 fusion.34
  216.6 1.4 fusion.82
  218.0 2.8 collective-permute-start.6
  222.5 2.2 collective-permute-done.6
  224.6 3.3 collective-permute-done.7
  228.3 2.3 convolution_bitcast_fusion
  230.6 4.0 reshape.636
  234.6 5.0 convolution_bitcast_fusion.3
  240.1 80.5 %psum.23 = f32[8,17,17]{2,1,0:T(8,128)S(1)} all-reduce(f32[8,17,17]{2,1,0:T(8,128)S(1)} %convolution_bitcast_fusion.5), channel_id=1, replica_groups=mesh['az'=8,'rng'=8,'dp'=4] {'az','rng','dp'}, use_global_device_ids=true, to_apply=%region_6.7 | all-reduce | flops 2312 | bytes 18496 | tf_op jit(solution)/shard_map/psum | solution.py:222
  322.5 183.8 %all-reduce.3.cloned.1.call-done = (f32[512,1536]{0,1:T(8,128)}, f32[512,512]{1,0:T(8,128)}) async-done(((f32[512,1536]{0,1:T(8,128)}, f32[512,512]{1,0:T(8,128)}), (f32[512,1536]{0,1:T(8,128)}, f32[512,512]{1,0:T(8,128)})) %all-reduce.3.cloned.1.call-update) | async-done | bytes 4194320 | tf_op jit(solution)/shard_map/psum | solution.py:222
  506.3 1.4 constant_dynamic-slice_fusion.4
  (141 shorter events, 58.0 us)
Async XLA Ops:
  7.2 1.4 copy-start
  7.2 16.1 %copy-start.14 = (bf16[1,16,16,512]{3,2,1,0:T(8,128)(2,1)S(1)}, bf16[1,16,16,512]{3,2,1,0:T(8,128)(2,1)}, u32[]{:S(2)}) copy-start(bf16[1,16,16,512]{3,2,1,0:T(8,128)(2,1)} %param.17) | copy-start | bytes 786436
  7.2 499.1 %all-reduce.3.cloned.1.call-start = ((), (), s32[]{:S(2)}) async-start(), calls=%async_computation | async-start | bytes 8388608 | tf_op jit(solution)/shard_map/psum | solution.py:222
  11.0 36.4 %collective-permute-start = (bf16[1,8,16,1024]{3,2,1,0:T(8,128)(2,1)}, bf16[1,8,16,1024]{3,2,1,0:T(8,128)(2,1)}, u32[]{:S(2)}, u32[]{:S(2)}) collective-permute-start(bf16[1,8,16,1024]{3,2,1,0:T(8,128)(2,1)} %get-tuple-element.161), channel_id=1, source_target_pairs={{0,32},{32,64},{64,96},{96,128},{128,160},{160,192},{192,224},{224... | collective-permute-start | bytes 786440 | tf_op jit(solution)/shard_map/ppermute | solution.py:16
  13.8 33.6 %collective-permute-start.1 = (bf16[1,8,16,1024]{3,2,1,0:T(8,128)(2,1)}, bf16[1,8,16,1024]{3,2,1,0:T(8,128)(2,1)}, u32[]{:S(2)}, u32[]{:S(2)}) collective-permute-start(bf16[1,8,16,1024]{3,2,1,0:T(8,128)(2,1)} %get-tuple-element.162), channel_id=1, source_target_pairs={{32,0},{64,32},{96,64},{128,96},{160,128},{192,160},{224,192},{0,2... | collective-permute-start | bytes 786440 | tf_op jit(solution)/shard_map/ppermute | solution.py:18
  22.3 25.1 %copy-start.9 = (bf16[1,16,16,1024]{3,2,1,0:T(8,128)(2,1)}, bf16[1,16,16,1024]{3,2,1,0:T(8,128)(2,1)S(1)}, u32[]{:S(2)}) copy-start(bf16[1,16,16,1024]{3,2,1,0:T(8,128)(2,1)S(1)} %slice.310) | copy-start | bytes 1572868
  34.2 12.6 %copy-start.19 = (f32[8,17,17]{2,0,1:T(8,128)S(1)}, f32[8,17,17]{2,0,1:T(8,128)}, u32[]{:S(2)}) copy-start(f32[8,17,17]{2,0,1:T(8,128)} %param.16) | copy-start | bytes 27748
  49.6 20.4 %collective-permute-start.2 = (bf16[1,32,8,1024]{3,2,1,0:T(8,128)(2,1)}, bf16[1,32,8,1024]{3,2,1,0:T(8,128)(2,1)}, u32[]{:S(2)}, u32[]{:S(2)}) collective-permute-start(bf16[1,32,8,1024]{3,2,1,0:T(8,128)(2,1)} %get-tuple-element.159), channel_id=1, source_target_pairs={{0,4},{4,8},{8,12},{12,16},{16,20},{20,24},{24,28},{28,0},{1,5},{5... | collective-permute-start | bytes 1572872 | tf_op jit(solution)/shard_map/ppermute | solution.py:16
  50.8 19.2 %collective-permute-start.3 = (bf16[1,32,8,1024]{3,2,1,0:T(8,128)(2,1)}, bf16[1,32,8,1024]{3,2,1,0:T(8,128)(2,1)}, u32[]{:S(2)}, u32[]{:S(2)}) collective-permute-start(bf16[1,32,8,1024]{3,2,1,0:T(8,128)(2,1)} %get-tuple-element.160), channel_id=1, source_target_pairs={{4,0},{8,4},{12,8},{16,12},{20,16},{24,20},{28,24},{0,28},{5,1},{9... | collective-permute-start | bytes 1572872 | tf_op jit(solution)/shard_map/ppermute | solution.py:18
  128.9 1.5 copy-start.10
  130.4 1.7 copy-start.3
  130.4 2.0 copy-start.11
  136.6 1.6 copy-start.2
  186.0 1.7 copy-start.5
  187.6 1.7 copy-start.7
  189.3 1.7 copy-start.8
  191.0 1.7 copy-start.6
  193.2 6.0 %copy-start.1 = (f32[1,32,32,1024]{3,2,1,0:T(8,128)}, f32[1,32,32,1024]{3,2,1,0:T(8,128)S(1)}, u32[]{:S(2)}) copy-start(f32[1,32,32,1024]{3,2,1,0:T(8,128)S(1)} %add_dynamic-update-slice_fusion) | copy-start | bytes 12582916
  193.3 5.9 %copy-start.12 = (bf16[4,8,64,64]{3,2,1,0:T(8,128)(2,1)S(1)}, bf16[4,8,64,64]{3,2,1,0:T(8,128)(2,1)}, u32[]{:S(2)}) copy-start(bf16[4,8,64,64]{3,2,1,0:T(8,128)(2,1)} %get-tuple-element.172) | copy-start | bytes 786436
  194.4 17.1 %collective-permute-start.4 = (bf16[1,32,8,1024]{3,2,1,0:T(8,128)(2,1)}, bf16[1,32,8,1024]{3,2,1,0:T(8,128)(2,1)}, u32[]{:S(2)}, u32[]{:S(2)}) collective-permute-start(bf16[1,32,8,1024]{3,2,1,0:T(8,128)(2,1)} %get-tuple-element.155), channel_id=1, source_target_pairs={{0,4},{4,8},{8,12},{12,16},{16,20},{20,24},{24,28},{1,5},{5,9},{9,... | collective-permute-start | bytes 1572872 | tf_op jit(solution)/shard_map/ppermute | solution.py:16
  196.5 15.0 %collective-permute-start.5 = (bf16[1,32,8,1024]{3,2,1,0:T(8,128)(2,1)}, bf16[1,32,8,1024]{3,2,1,0:T(8,128)(2,1)}, u32[]{:S(2)}, u32[]{:S(2)}) collective-permute-start(bf16[1,32,8,1024]{3,2,1,0:T(8,128)(2,1)} %get-tuple-element.156), channel_id=1, source_target_pairs={{4,0},{8,4},{12,8},{16,12},{20,16},{24,20},{28,24},{5,1},{9,5},{13... | collective-permute-start | bytes 1572872 | tf_op jit(solution)/shard_map/ppermute | solution.py:18
  210.1 18.2 %copy-start.17 = (bf16[1,2,8,2,8,512]{5,4,3,2,1,0:T(8,128)(2,1)}, bf16[1,2,8,2,8,512]{5,4,3,2,1,0:T(8,128)(2,1)S(1)}, u32[]{:S(2)}) copy-start(bf16[1,2,8,2,8,512]{5,4,3,2,1,0:T(8,128)(2,1)S(1)} %copy.26) | copy-start | bytes 786436
  214.0 7.0 %copy-start.13 = (bf16[1,2,8,2,8,512]{5,4,3,2,1,0:T(8,128)(2,1)S(1)}, bf16[1,2,8,2,8,512]{5,4,3,2,1,0:T(8,128)(2,1)}, u32[]{:S(2)}) copy-start(bf16[1,2,8,2,8,512]{5,4,3,2,1,0:T(8,128)(2,1)} %copy.35) | copy-start | bytes 786436
  214.0 7.0 %copy-start.15 = (bf16[1,16,16,512]{3,2,1,0:T(8,128)(2,1)S(1)}, bf16[1,16,16,512]{3,2,1,0:T(8,128)(2,1)}, u32[]{:S(2)}) copy-start(bf16[1,16,16,512]{3,2,1,0:T(8,128)(2,1)} %param.17) | copy-start | bytes 786436
  216.6 5.7 %copy-start.4 = (f32[1,32,16,1024]{3,2,1,0:T(8,128)S(1)}, f32[1,32,16,1024]{3,2,1,0:T(8,128)}, u32[]{:S(2)}) copy-start(f32[1,32,16,1024]{3,2,1,0:T(8,128)} %fusion.34) | copy-start | bytes 6291460
  218.0 6.6 %collective-permute-start.6 = (bf16[1,8,16,1024]{3,2,1,0:T(8,128)(2,1)S(1)}, bf16[1,8,16,1024]{3,2,1,0:T(8,128)(2,1)S(1)}, u32[]{:S(2)}, u32[]{:S(2)}) collective-permute-start(bf16[1,8,16,1024]{3,2,1,0:T(8,128)(2,1)S(1)} %get-tuple-element.157), channel_id=1, source_target_pairs={{0,32},{32,64},{64,96},{96,128},{128,160},{160,192},{192,224},{224... | collective-permute-start | bytes 786440 | tf_op jit(solution)/shard_map/ppermute | solution.py:16
  220.8 7.2 %collective-permute-start.7 = (bf16[1,8,16,1024]{3,2,1,0:T(8,128)(2,1)S(1)}, bf16[1,8,16,1024]{3,2,1,0:T(8,128)(2,1)S(1)}, u32[]{:S(2)}, u32[]{:S(2)}) collective-permute-start(bf16[1,8,16,1024]{3,2,1,0:T(8,128)(2,1)S(1)} %get-tuple-element.158), channel_id=1, source_target_pairs={{32,0},{64,32},{96,64},{128,96},{160,128},{192,160},{224,192},{0,2... | collective-permute-start | bytes 786440 | tf_op jit(solution)/shard_map/ppermute | solution.py:18
  222.5 5.8 %copy-start.16 = (bf16[1,16,16,512]{3,2,1,0:T(8,128)(2,1)S(1)}, bf16[1,16,16,512]{3,2,1,0:T(8,128)(2,1)}, u32[]{:S(2)}) copy-start(bf16[1,16,16,512]{3,2,1,0:T(8,128)(2,1)} %param.13) | copy-start | bytes 786436
  234.6 86.6 %copy-start.18 = (bf16[1,2,8,2,8,512]{5,4,3,2,1,0:T(8,128)(2,1)S(1)}, bf16[1,2,8,2,8,512]{5,4,3,2,1,0:T(8,128)(2,1)}, u32[]{:S(2)}) copy-start(bf16[1,2,8,2,8,512]{5,4,3,2,1,0:T(8,128)(2,1)} %copy-done.17) | copy-start | bytes 786436
Sparse Core Ops, SparseCore 0:
  230.7 275.5 all-reduce.2
where the time goes:
time: 525 us; the launch traced here: 517 us
  waiting for transfers between devices  189 us (36%)
  local copies, waits for them, and re-layouts  158 us (30%)
  blocking collectives  80.5 us (15%)
  matrix products  32.1 us (6%)
  between operations  22.6 us (4%)
  other arithmetic  21 us (4%)
  starting transfers between devices  13.2 us (3%)
    psum x1, waiting for transfers between devices, shards(): lax.psum((local_qkv, local_out, bias_local), ('az', 'rng', 'dp'))  184 us
    psum x1, blocking collectives, shards(): lax.psum((local_qkv, local_out, bias_local), ('az', 'rng', 'dp'))  80.5 us
    gather x36, local copies, waits for them, and re-layouts  35.3 us
    unnamed x47, local copies, waits for them, and re-layouts  24.1 us
    slice x4, local copies, waits for them, and re-layouts, query_turn(): terms[member]  23.1 us
    squeeze x4, local copies, waits for them, and re-layouts, query_turn(): terms[member]  20.1 us
    reshape x1, local copies, waits for them, and re-layouts, query_tile(): lax.dynamic_slice(key_ext, place, (1, ext_side, ext_side, 2 * width))  13.1 us
  transfers between devices with their start and end apart: 9, of which 3 were waited for; matrix products, arithmetic and copies ran while one was open for 13% of the time, Pallas kernels for 0%

commit v1 on v0

--- a/solution.py
+++ b/solution.py
@@ -220,7 +220,7 @@
     )
     share = width // (lax.axis_size("az") * lax.axis_size("rng"))
     total_qkv, total_out, total_bias = lax.psum(
-        (local_qkv, local_out, bias_local), ("az", "rng", "dp")
+        lax.psum((local_qkv, local_out, bias_local), "az"), ("rng", "dp")
     )
     first_row = lax.axis_index(("az", "rng")) * share
     rows_qkv = lax.dynamic_slice_in_dim(total_qkv, first_row, share, 0)

time: 525 us -> 527 us (level)
  the two profiles are of different devices: /device:TPU:97 before, /device:TPU:64 now
where the time goes in v1:
time: 527 us; the launch traced here: 519 us
  local copies, waits for them, and re-layouts  158 us (30%)
  blocking collectives  155 us (29%)
  waiting for transfers between devices  117 us (22%)
  matrix products  32 us (6%)
  between operations  22.8 us (4%)
  other arithmetic  21.2 us (4%)
  starting transfers between devices  13.4 us (3%)
    psum x1, blocking collectives, shards(): lax.psum(lax.psum((local_qkv, local_out, bias_local), 'az'), ('rng', 'dp'))  124 us
    psum x1, waiting for transfers between devices, shards(): lax.psum((local_qkv, local_out, bias_local), 'az')  110 us
    gather x36, local copies, waits for them, and re-layouts  35.6 us
    psum x1, blocking collectives, shards(): lax.psum((local_qkv, local_out, bias_local), 'az')  30.6 us
    unnamed x47, local copies, waits for them, and re-layouts  24.1 us
    slice x4, local copies, waits for them, and re-layouts, query_turn(): terms[member]  23.1 us
    squeeze x4, local copies, waits for them, and re-layouts, query_turn(): terms[member]  20.1 us
    reshape x1, local copies, waits for them, and re-layouts, query_tile(): lax.dynamic_slice(key_ext, place, (1, ext_side, ext_side, 2 * width))  13.1 us
  transfers between devices with their start and end apart: 10, of which 3 were waited for; matrix products, arithmetic and copies ran while one was open for 13% of the time, Pallas kernels for 0%

profile of v1, /device:TPU:64, one launch (start us, length us, event | category | flops | bytes accessed | tf_op | source)
XLA Modules:
  0.0 519.2 jit_solution(2141939533824838888)
XLA Ops:
  8.6 1.5 convolution_convert_fusion
  11.0 1.9 collective-permute-start
  24.1 8.4 %while.16 = (s32[]{:T(128)}, bf16[1,16,16,512]{3,2,1,0:T(8,128)(2,1)S(1)}, s32[4,4]{1,0:T(4,128)S(1)}, bf16[4,1,8,8,512]{4,3,2,1,0:T(8,128)(2,1)S(1)}, s32[]{:T(128)}) while((s32[]{:T(128)}, bf16[1,16,16,512]{3,2,1,0:T(8,128)(2,1)S(1)}, s32[4,4]{1,0:T(4,128)S(1)}, bf16[4,1,8,8,512]{4,3,2,1,0:T(8,128)(2,1)S(1)}, s32[]{:T(128)}) %tuple.104), condition=%wide.while_cond.6, body=%wide.while_body.6.sunk | while | flops 2 | bytes 131205 | solution.py:138
  33.9 8.2 %while.15 = (s32[]{:T(128)}, bf16[1,16,16,512]{3,2,1,0:T(8,128)(2,1)S(1)}, s32[4,4]{1,0:T(4,128)S(1)}, bf16[4,1,8,8,512]{4,3,2,1,0:T(8,128)(2,1)S(1)}, s32[]{:T(128)}) while((s32[]{:T(128)}, bf16[1,16,16,512]{3,2,1,0:T(8,128)(2,1)S(1)}, s32[4,4]{1,0:T(4,128)S(1)}, bf16[4,1,8,8,512]{4,3,2,1,0:T(8,128)(2,1)S(1)}, s32[]{:T(128)}) %tuple.105), condition=%wide.while_cond.5, body=%wide.while_body.5.sunk | while | flops 2 | bytes 131205 | solution.py:135
  43.2 2.6 copy.46
  49.2 1.5 collective-permute-start.2
  50.7 3.1 collective-permute-start.3
  53.8 4.6 convolution_bitcast_fusion.1
  58.4 6.6 %copy.22 = f32[8,8,8,24,24]{4,3,2,1,0:T(8,128)} copy(f32[8,8,8,24,24]{3,4,1,2,0:T(8,128)} %convolution_bitcast_fusion.1) | data formatting | bytes 2359296 | tf_op jit(solution)/shard_map/ikx,hxjl->hijkl/transpose | solution.py:40
  65.0 4.3 add.393
  70.1 2.8 pad_maximum_fusion.1
  72.9 19.3 %while.14 = (s32[]{:T(128)}, bf16[1,32,32,1024]{3,2,1,0:T(8,128)(2,1)}, s32[4,4]{1,0:T(4,128)S(1)}, bf16[4,1,24,24,1024]{4,3,2,1,0:T(8,128)(2,1)}, s32[]{:T(128)}) while((s32[]{:T(128)}, bf16[1,32,32,1024]{3,2,1,0:T(8,128)(2,1)}, s32[4,4]{1,0:T(4,128)S(1)}, bf16[4,1,24,24,1024]{4,3,2,1,0:T(8,128)(2,1)}, s32[]{:T(128)}) %tuple.95), condition=%wide.while_cond.4, body=%wide.while_body.4.sunk | while | flops 2 | bytes 2360445 | solution.py:141
  73.5 4.3 bitcast_dynamic-update-slice_fusion.6
  78.4 4.2 bitcast_dynamic-update-slice_fusion.6
  83.2 4.3 bitcast_dynamic-update-slice_fusion.6
  88.1 4.2 bitcast_dynamic-update-slice_fusion.6
  92.2 13.1 %reshape.627 = bf16[4,576,2,8,64]{4,3,2,1,0:T(8,128)(2,1)} reshape(bf16[4,1,24,24,1024]{4,3,2,1,0:T(8,128)(2,1)} %get-tuple-element.92) | data formatting | bytes 9437184 | tf_op jit(solution)/shard_map/while/body/eval_jaxpr/vmap()/reshape | solution.py:141
  105.3 8.1 %fusion.80 = (bf16[4,576,1,8,64]{4,3,2,1,0:T(8,128)(2,1)}, bf16[4,576,1,8,64]{4,3,2,1,0:T(8,128)(2,1)}) fusion(bf16[4,576,2,8,64]{4,3,2,1,0:T(8,128)(2,1)} %reshape.627), kind=kLoop, calls=%fused_computation.139 | loop fusion | bytes 9437184 | tf_op jit(solution)/shard_map/while/body/eval_jaxpr/vmap()/slice | solution.py:146
  113.5 6.2 %copy.51 = bf16[4,576,1,8,64]{1,4,3,0,2:T(8,128)(2,1)} copy(bf16[4,576,1,8,64]{4,3,2,1,0:T(8,128)(2,1)} %get-tuple-element.155) | data formatting | bytes 4718592
  119.7 6.2 %copy.50 = bf16[4,576,1,8,64]{1,4,3,0,2:T(8,128)(2,1)} copy(bf16[4,576,1,8,64]{4,3,2,1,0:T(8,128)(2,1)} %get-tuple-element.156) | data formatting | bytes 4718592
  125.9 3.1 fusion.86
  129.1 1.5 exponential_reduce_fusion
  132.6 2.1 multiply_reduce_fusion
  134.7 2.1 fusion.87
  138.3 4.6 pad_maximum_fusion
  142.9 5.8 %copy.32 = f32[1,576,2,8,64]{4,3,2,1,0:T(8,128)} copy(f32[1,576,2,8,64]{1,4,3,0,2:T(8,128)} %get-tuple-element.151) | data formatting | bytes 4718592 | tf_op jit(solution)/shard_map/while/body/eval_jaxpr/slice | solution.py:178
  148.7 5.0 squeeze.52
  153.7 5.8 %copy.29 = f32[1,576,2,8,64]{4,3,2,1,0:T(8,128)} copy(f32[1,576,2,8,64]{1,4,3,0,2:T(8,128)} %get-tuple-element.152) | data formatting | bytes 4718592 | tf_op jit(solution)/shard_map/while/body/eval_jaxpr/slice | solution.py:178
  159.5 5.0 squeeze.45
  164.5 5.8 %copy.30 = f32[1,576,2,8,64]{4,3,2,1,0:T(8,128)} copy(f32[1,576,2,8,64]{1,4,3,0,2:T(8,128)} %get-tuple-element.153) | data formatting | bytes 4718592 | tf_op jit(solution)/shard_map/while/body/eval_jaxpr/slice | solution.py:178
  170.3 5.0 squeeze.48
  175.3 5.8 %copy.31 = f32[1,576,2,8,64]{4,3,2,1,0:T(8,128)} copy(f32[1,576,2,8,64]{1,4,3,0,2:T(8,128)} %get-tuple-element.154) | data formatting | bytes 4718592 | tf_op jit(solution)/shard_map/while/body/eval_jaxpr/slice | solution.py:178
  181.1 5.0 squeeze.50
  194.5 2.1 collective-permute-start.4
  198.0 1.4 slice.323
  202.6 4.3 fusion.29
  211.7 2.6 fusion.35
  214.3 2.6 fusion.34
  216.9 1.4 fusion.82
  218.3 3.1 collective-permute-start.6
  223.2 3.0 collective-permute-done.6
  226.2 3.6 collective-permute-done.7
  230.1 2.3 convolution_bitcast_fusion
  232.4 110.1 %all-reduce.7.cloned.1.call-done = (f32[512,1536]{0,1:T(8,128)}, f32[512,512]{1,0:T(8,128)}) async-done(((f32[512,1536]{0,1:T(8,128)}, f32[512,512]{1,0:T(8,128)}), (f32[512,1536]{0,1:T(8,128)}, f32[512,512]{1,0:T(8,128)})) %all-reduce.7.cloned.1.call-update) | async-done | bytes 4194320 | tf_op jit(solution)/shard_map/psum | solution.py:223
  342.5 4.0 reshape.636
  346.5 5.0 convolution_bitcast_fusion.3
  352.0 30.6 %psum.46 = f32[8,17,17]{2,1,0:T(8,128)S(1)} all-reduce(f32[8,17,17]{2,1,0:T(8,128)S(1)} %convolution_bitcast_fusion.5), channel_id=1, replica_groups=mesh['az'=8,'rng'=8,'dp'=4] {'az'}, use_global_device_ids=true, to_apply=%region_8.9 | all-reduce | flops 2312 | bytes 18496 | tf_op jit(solution)/shard_map/psum | solution.py:223
  382.6 124.0 %psum.47 = f32[8,17,17]{2,1,0:T(8,128)S(1)} all-reduce(f32[8,17,17]{2,1,0:T(8,128)S(1)} %psum.46), channel_id=1, replica_groups=mesh['az'=8,'rng'=8,'dp'=4] {'rng','dp'}, use_global_device_ids=true, to_apply=%region_9.10 | all-reduce | flops 2312 | bytes 18496 | tf_op jit(solution)/shard_map/psum | solution.py:222
  (145 shorter events, 60.0 us)
Async XLA Ops:
  7.2 1.4 copy-start
  7.2 15.4 %copy-start.14 = (bf16[1,16,16,512]{3,2,1,0:T(8,128)(2,1)S(1)}, bf16[1,16,16,512]{3,2,1,0:T(8,128)(2,1)}, u32[]{:S(2)}) copy-start(bf16[1,16,16,512]{3,2,1,0:T(8,128)(2,1)} %param.17) | copy-start | bytes 786436
  7.2 335.3 %all-reduce.7.cloned.1.call-start = ((), (), s32[]{:S(2)}) async-start(), calls=%async_computation.1 | async-start | bytes 8388608 | tf_op jit(solution)/shard_map/psum | solution.py:223
  11.0 36.0 %collective-permute-start = (bf16[1,8,16,1024]{3,2,1,0:T(8,128)(2,1)}, bf16[1,8,16,1024]{3,2,1,0:T(8,128)(2,1)}, u32[]{:S(2)}, u32[]{:S(2)}) collective-permute-start(bf16[1,8,16,1024]{3,2,1,0:T(8,128)(2,1)} %get-tuple-element.163), channel_id=1, source_target_pairs={{0,32},{32,64},{64,96},{96,128},{128,160},{160,192},{192,224},{224... | collective-permute-start | bytes 786440 | tf_op jit(solution)/shard_map/ppermute | solution.py:16
  12.9 34.1 %collective-permute-start.1 = (bf16[1,8,16,1024]{3,2,1,0:T(8,128)(2,1)}, bf16[1,8,16,1024]{3,2,1,0:T(8,128)(2,1)}, u32[]{:S(2)}, u32[]{:S(2)}) collective-permute-start(bf16[1,8,16,1024]{3,2,1,0:T(8,128)(2,1)} %get-tuple-element.164), channel_id=1, source_target_pairs={{32,0},{64,32},{96,64},{128,96},{160,128},{192,160},{224,192},{0,2... | collective-permute-start | bytes 786440 | tf_op jit(solution)/shard_map/ppermute | solution.py:18
  21.6 25.3 %copy-start.9 = (bf16[1,16,16,1024]{3,2,1,0:T(8,128)(2,1)}, bf16[1,16,16,1024]{3,2,1,0:T(8,128)(2,1)S(1)}, u32[]{:S(2)}) copy-start(bf16[1,16,16,1024]{3,2,1,0:T(8,128)(2,1)S(1)} %slice.310) | copy-start | bytes 1572868
  33.9 12.5 %copy-start.19 = (f32[8,17,17]{2,0,1:T(8,128)S(1)}, f32[8,17,17]{2,0,1:T(8,128)}, u32[]{:S(2)}) copy-start(f32[8,17,17]{2,0,1:T(8,128)} %param.16) | copy-start | bytes 27748
  49.2 20.9 %collective-permute-start.2 = (bf16[1,32,8,1024]{3,2,1,0:T(8,128)(2,1)}, bf16[1,32,8,1024]{3,2,1,0:T(8,128)(2,1)}, u32[]{:S(2)}, u32[]{:S(2)}) collective-permute-start(bf16[1,32,8,1024]{3,2,1,0:T(8,128)(2,1)} %get-tuple-element.161), channel_id=1, source_target_pairs={{0,4},{4,8},{8,12},{12,16},{16,20},{20,24},{24,28},{28,0},{1,5},{5... | collective-permute-start | bytes 1572872 | tf_op jit(solution)/shard_map/ppermute | solution.py:16
  50.7 19.4 %collective-permute-start.3 = (bf16[1,32,8,1024]{3,2,1,0:T(8,128)(2,1)}, bf16[1,32,8,1024]{3,2,1,0:T(8,128)(2,1)}, u32[]{:S(2)}, u32[]{:S(2)}) collective-permute-start(bf16[1,32,8,1024]{3,2,1,0:T(8,128)(2,1)} %get-tuple-element.162), channel_id=1, source_target_pairs={{4,0},{8,4},{12,8},{16,12},{20,16},{24,20},{28,24},{0,28},{5,1},{9... | collective-permute-start | bytes 1572872 | tf_op jit(solution)/shard_map/ppermute | solution.py:18
  129.1 1.5 copy-start.10
  130.6 1.7 copy-start.3
  130.6 2.0 copy-start.11
  136.8 1.6 copy-start.2
  186.1 1.7 copy-start.5
  187.8 1.7 copy-start.7
  189.5 1.7 copy-start.8
  191.1 1.7 copy-start.6
  193.4 6.0 %copy-start.1 = (f32[1,32,32,1024]{3,2,1,0:T(8,128)}, f32[1,32,32,1024]{3,2,1,0:T(8,128)S(1)}, u32[]{:S(2)}) copy-start(f32[1,32,32,1024]{3,2,1,0:T(8,128)S(1)} %add_dynamic-update-slice_fusion) | copy-start | bytes 12582916
  193.4 6.0 %copy-start.12 = (bf16[4,8,64,64]{3,2,1,0:T(8,128)(2,1)S(1)}, bf16[4,8,64,64]{3,2,1,0:T(8,128)(2,1)}, u32[]{:S(2)}) copy-start(bf16[4,8,64,64]{3,2,1,0:T(8,128)(2,1)} %get-tuple-element.174) | copy-start | bytes 786436
  194.5 17.1 %collective-permute-start.4 = (bf16[1,32,8,1024]{3,2,1,0:T(8,128)(2,1)}, bf16[1,32,8,1024]{3,2,1,0:T(8,128)(2,1)}, u32[]{:S(2)}, u32[]{:S(2)}) collective-permute-start(bf16[1,32,8,1024]{3,2,1,0:T(8,128)(2,1)} %get-tuple-element.157), channel_id=1, source_target_pairs={{0,4},{4,8},{8,12},{12,16},{16,20},{20,24},{24,28},{1,5},{5,9},{9,... | collective-permute-start | bytes 1572872 | tf_op jit(solution)/shard_map/ppermute | solution.py:16
  196.7 15.0 %collective-permute-start.5 = (bf16[1,32,8,1024]{3,2,1,0:T(8,128)(2,1)}, bf16[1,32,8,1024]{3,2,1,0:T(8,128)(2,1)}, u32[]{:S(2)}, u32[]{:S(2)}) collective-permute-start(bf16[1,32,8,1024]{3,2,1,0:T(8,128)(2,1)} %get-tuple-element.158), channel_id=1, source_target_pairs={{4,0},{8,4},{12,8},{16,12},{20,16},{24,20},{28,24},{5,1},{9,5},{13... | collective-permute-start | bytes 1572872 | tf_op jit(solution)/shard_map/ppermute | solution.py:18
  210.2 19.8 %copy-start.17 = (bf16[1,2,8,2,8,512]{5,4,3,2,1,0:T(8,128)(2,1)}, bf16[1,2,8,2,8,512]{5,4,3,2,1,0:T(8,128)(2,1)S(1)}, u32[]{:S(2)}) copy-start(bf16[1,2,8,2,8,512]{5,4,3,2,1,0:T(8,128)(2,1)S(1)} %copy.26) | copy-start | bytes 786436
  214.3 7.4 %copy-start.13 = (bf16[1,2,8,2,8,512]{5,4,3,2,1,0:T(8,128)(2,1)S(1)}, bf16[1,2,8,2,8,512]{5,4,3,2,1,0:T(8,128)(2,1)}, u32[]{:S(2)}) copy-start(bf16[1,2,8,2,8,512]{5,4,3,2,1,0:T(8,128)(2,1)} %copy.35) | copy-start | bytes 786436
  214.3 7.4 %copy-start.15 = (bf16[1,16,16,512]{3,2,1,0:T(8,128)(2,1)S(1)}, bf16[1,16,16,512]{3,2,1,0:T(8,128)(2,1)}, u32[]{:S(2)}) copy-start(bf16[1,16,16,512]{3,2,1,0:T(8,128)(2,1)} %param.17) | copy-start | bytes 786436
  216.9 6.1 %copy-start.4 = (f32[1,32,16,1024]{3,2,1,0:T(8,128)S(1)}, f32[1,32,16,1024]{3,2,1,0:T(8,128)}, u32[]{:S(2)}) copy-start(f32[1,32,16,1024]{3,2,1,0:T(8,128)} %fusion.34) | copy-start | bytes 6291460
  218.3 7.8 %collective-permute-start.6 = (bf16[1,8,16,1024]{3,2,1,0:T(8,128)(2,1)S(1)}, bf16[1,8,16,1024]{3,2,1,0:T(8,128)(2,1)S(1)}, u32[]{:S(2)}, u32[]{:S(2)}) collective-permute-start(bf16[1,8,16,1024]{3,2,1,0:T(8,128)(2,1)S(1)} %get-tuple-element.159), channel_id=1, source_target_pairs={{0,32},{32,64},{64,96},{96,128},{128,160},{160,192},{192,224},{224... | collective-permute-start | bytes 786440 | tf_op jit(solution)/shard_map/ppermute | solution.py:16
  221.5 8.3 %collective-permute-start.7 = (bf16[1,8,16,1024]{3,2,1,0:T(8,128)(2,1)S(1)}, bf16[1,8,16,1024]{3,2,1,0:T(8,128)(2,1)S(1)}, u32[]{:S(2)}, u32[]{:S(2)}) collective-permute-start(bf16[1,8,16,1024]{3,2,1,0:T(8,128)(2,1)S(1)} %get-tuple-element.160), channel_id=1, source_target_pairs={{32,0},{64,32},{96,64},{128,96},{160,128},{192,160},{224,192},{0,2... | collective-permute-start | bytes 786440 | tf_op jit(solution)/shard_map/ppermute | solution.py:18
  223.1 6.9 %copy-start.16 = (bf16[1,16,16,512]{3,2,1,0:T(8,128)(2,1)S(1)}, bf16[1,16,16,512]{3,2,1,0:T(8,128)(2,1)}, u32[]{:S(2)}) copy-start(bf16[1,16,16,512]{3,2,1,0:T(8,128)(2,1)} %param.13) | copy-start | bytes 786436
  232.4 276.2 %all-reduce.5.cloned.1.call-start = ((), (), s32[]{:S(2)}) async-start(), calls=%async_computation | async-start | bytes 8388608 | tf_op jit(solution)/shard_map/psum | solution.py:222
  346.5 160.7 %copy-start.18 = (bf16[1,2,8,2,8,512]{5,4,3,2,1,0:T(8,128)(2,1)S(1)}, bf16[1,2,8,2,8,512]{5,4,3,2,1,0:T(8,128)(2,1)}, u32[]{:S(2)}) copy-start(bf16[1,2,8,2,8,512]{5,4,3,2,1,0:T(8,128)(2,1)} %copy-done.17) | copy-start | bytes 786436
Sparse Core Ops, SparseCore 0:
  232.5 109.9 all-reduce.6
  345.8 122.1 all-reduce.4
